TPU v7x, 32 devices: a whole 2x2x4 slice. The times are simulated.
32 devices in a mesh: wide: 8 (over z, x), narrow: 4 (over y, core).
Axes of the slice: x: 2, y: 2, z: 4, core: 2. Of those that a mesh axis runs over, the one named last changes fastest.
Arguments:
- tokens: bfloat16 [64, 512, 768], P(('wide', 'narrow')), may hold values from -6 to 6
- doc_lengths: int32 [64], P(('wide', 'narrow')), may hold values from 30 to 512
- qkv_weight: bfloat16 [768, 2304], replicated, may hold values from -0.21875 to 0.21875
- query_bias: bfloat16 [768], replicated, may hold values from -3 to 3
- value_bias: bfloat16 [768], replicated, may hold values from -3 to 3
- out_weight: bfloat16 [768, 768], replicated, may hold values from -0.625 to 0.625
- out_bias: bfloat16 [768], replicated, may hold values from -1.75 to 1.75
- first_gain: bfloat16 [768], replicated, may hold values from 0.5 to 1.5
- first_shift: bfloat16 [768], replicated, may hold values from -1.75 to 1.75
- up_weight: bfloat16 [768, 3072], replicated, may hold values from -0.21875 to 0.21875
- up_bias: bfloat16 [3072], replicated, may hold values from -3 to 3
- down_weight: bfloat16 [3072, 768], replicated, may hold values from -0.15625 to 0.15625
- down_bias: bfloat16 [768], replicated, may hold values from -1.75 to 1.75
- second_gain: bfloat16 [768], replicated, may hold values from 0.5 to 1.5
- second_shift: bfloat16 [768], replicated, may hold values from -1.75 to 1.75
- dir_weight: bfloat16 [1536, 8], replicated, may hold values from -0.375 to 0.375
- dir_bias: bfloat16 [8], replicated, may hold values from -1 to 1
- segment_rows: int32 [64, 128], P(('wide', 'narrow')), may hold values from 0 to 511, as said below
- segment_slots: int32 [32, 256], P(('wide', 'narrow')), may hold values from 0 to 255, each once within a row
- pair_rows: int32 [32, 256, 2], P(('wide', 'narrow')), may hold values from 0 to 255
- pair_labels: int32 [32, 256], P(('wide', 'narrow')), may hold values from 0 to 7
- out_cotangent: bfloat16 [64, 512, 768], P(('wide', 'narrow')), may hold values from -6 to 6
Outputs:
- encoded: bfloat16 [64, 512, 768], P(('wide', 'narrow'))
- grad_tokens: bfloat16 [64, 512, 768], P(('wide', 'narrow'))
- grad_qkv_weight: float32 [768, 2304], P('narrow', 'wide')
- grad_query_bias: float32 [768], replicated
- grad_value_bias: float32 [768], replicated
- grad_out_weight: float32 [768, 768], P('narrow', 'wide')
- grad_out_bias: float32 [768], replicated
- grad_first_gain: float32 [768], replicated
- grad_first_shift: float32 [768], replicated
- grad_up_weight: float32 [768, 3072], P('narrow', 'wide')
- grad_up_bias: float32 [3072], replicated
- grad_down_weight: float32 [3072, 768], P('narrow', 'wide')
- grad_down_bias: float32 [768], replicated
- grad_second_gain: float32 [768], replicated
- grad_second_shift: float32 [768], replicated
- grad_dir_weight: float32 [1536, 8], replicated
- grad_dir_bias: float32 [8], replicated
Inputs may be any that keep to these rules, and one draw needn't show every extreme that they name: `segment_rows`: each value is below the token count of its document. `segment_slots`: each device's row holds every slot once.
All inputs are finite; a program needn't handle non-finite values.
Results may differ from a plain program's by a relative error of at most 0.02.
Values may be sent and summed in bfloat16 or wider, within the bound.
A program may use at most 192 MiB of HBM per device.

v0:
```python
import jax
import jax.numpy as jnp
from jax import lax
from jax.sharding import PartitionSpec as P

HEADS = 12
HEAD_DIM = 64
EXACT = lax.Precision.HIGHEST
MASKED = -1e30
EPSILON = 1e-05


def norm_forward(values, gain, shift):
    center = jnp.mean(values, -1, keepdims=True)
    centered = values - center
    inverse = lax.rsqrt(jnp.mean(centered * centered, -1, keepdims=True) + EPSILON)
    normed = centered * inverse
    return (normed * gain + shift, normed, inverse)


def norm_backward(grad, normed, inverse, gain):
    scaled = grad * gain
    first_mean = jnp.mean(scaled, -1, keepdims=True)
    second_mean = jnp.mean(scaled * normed, -1, keepdims=True)
    return (
        (scaled - first_mean - normed * second_mean) * inverse,
        jnp.sum(grad * normed, 0),
        jnp.sum(grad, 0),
    )


def normal_cdf(values):
    return 0.5 * (1.0 + lax.erf(values * 0.7071067811865476))


def on_device(
    tokens,
    doc_lengths,
    qkv_weight,
    query_bias,
    value_bias,
    out_weight,
    out_bias,
    first_gain,
    first_shift,
    up_weight,
    up_bias,
    down_weight,
    down_bias,
    second_gain,
    second_shift,
    dir_weight,
    dir_bias,
    segment_rows,
    segment_slots,
    pair_rows,
    pair_labels,
    out_cotangent,
):
    doc_count, length, model_width = tokens.shape
    score_scale = HEAD_DIM ** (-0.5)
    token_rows = tokens.reshape(doc_count * length, model_width)
    allowed = lax.broadcasted_iota(jnp.int32, (doc_count, length), 1) < doc_lengths[:, None]
    allowed_rows = allowed.reshape(-1, 1).astype(jnp.float32)
    bias_row = jnp.concatenate([query_bias, jnp.zeros_like(query_bias), value_bias]).astype(
        jnp.float32
    )
    qkv = (jnp.dot(token_rows, qkv_weight, preferred_element_type=jnp.float32) + bias_row).astype(
        jnp.bfloat16
    )

    def split_heads(doc_block, which):
        return doc_block[:, which * model_width : (which + 1) * model_width].reshape(
            length, HEADS, HEAD_DIM
        )

    def scores_of(queries, key_rows, doc_mask):
        scores = (
            jnp.einsum("qhd,khd->hqk", queries, key_rows, preferred_element_type=jnp.float32)
            * score_scale
        )
        return jnp.where(doc_mask[None, None, :], scores, MASKED)

    mixed_parts = []
    log_totals = []
    for doc_index in range(doc_count):
        doc_block = qkv[doc_index * length : (doc_index + 1) * length]
        queries = split_heads(doc_block, 0)
        key_rows = split_heads(doc_block, 1)
        value_rows = split_heads(doc_block, 2)
        scores = scores_of(queries, key_rows, allowed[doc_index])
        highest = jnp.max(scores, -1, keepdims=True)
        powers = jnp.exp(scores - highest)
        summed = jnp.sum(powers, -1, keepdims=True)
        attention = (powers / summed).astype(jnp.bfloat16)
        log_totals.append(highest + jnp.log(summed))
        mixed_parts.append(
            jnp.einsum(
                "hqk,khd->qhd", attention, value_rows, preferred_element_type=jnp.float32
            ).reshape(length, model_width)
        )
    mixed = jnp.concatenate(mixed_parts).astype(jnp.bfloat16)
    attended = jnp.dot(mixed, out_weight, preferred_element_type=jnp.float32) + out_bias.astype(
        jnp.float32
    )
    resid_one = token_rows.astype(jnp.float32) + attended
    hidden_one, normed_one, inverse_one = norm_forward(
        resid_one, first_gain.astype(jnp.float32), first_shift.astype(jnp.float32)
    )
    hidden_low = hidden_one.astype(jnp.bfloat16)
    upper_pre = jnp.dot(hidden_low, up_weight, preferred_element_type=jnp.float32) + up_bias.astype(
        jnp.float32
    )
    cumulative = normal_cdf(upper_pre)
    active = (upper_pre * cumulative).astype(jnp.bfloat16)
    lowered = jnp.dot(active, down_weight, preferred_element_type=jnp.float32) + down_bias.astype(
        jnp.float32
    )
    resid_two = hidden_one + lowered
    second_float = second_gain.astype(jnp.float32)
    normed_out, normed_two, inverse_two = norm_forward(
        resid_two, second_float, second_shift.astype(jnp.float32)
    )
    encoded_rows = (normed_out * allowed_rows).astype(jnp.bfloat16)
    doc_starts = lax.broadcasted_iota(jnp.int32, (doc_count, 1), 0) * length
    picked_rows = (segment_rows + doc_starts).reshape(-1)
    picked = encoded_rows[picked_rows]
    slots = segment_slots.reshape(-1)
    outgoing = jnp.zeros_like(picked).at[slots].set(picked)
    arrived = lax.all_to_all(outgoing, "wide", split_axis=0, concat_axis=0, tiled=True)
    pairs = pair_rows.reshape(-1, 2)
    labels = pair_labels.reshape(-1)
    first_rows = arrived[pairs[:, 0]]
    second_rows = arrived[pairs[:, 1]]
    logits = (
        jnp.dot(first_rows, dir_weight[:model_width], preferred_element_type=jnp.float32)
        + jnp.dot(second_rows, dir_weight[model_width:], preferred_element_type=jnp.float32)
        + dir_bias.astype(jnp.float32)
    )
    powers_head = jnp.exp(logits - jnp.max(logits, -1, keepdims=True))
    chance = powers_head / jnp.sum(powers_head, -1, keepdims=True)
    classes = lax.broadcasted_iota(jnp.int32, logits.shape, 1)
    delta = chance - (labels[:, None] == classes).astype(jnp.float32)
    first_float = first_rows.astype(jnp.float32)
    second_rows_float = second_rows.astype(jnp.float32)
    grad_dir_weight = jnp.concatenate(
        [
            jnp.dot(first_float.T, delta, precision=EXACT, preferred_element_type=jnp.float32),
            jnp.dot(
                second_rows_float.T, delta, precision=EXACT, preferred_element_type=jnp.float32
            ),
        ]
    )
    grad_dir_bias = jnp.sum(delta, 0)
    dir_float = dir_weight.astype(jnp.float32)
    grad_first = jnp.dot(
        delta, dir_float[:model_width].T, precision=EXACT, preferred_element_type=jnp.float32
    )
    grad_second = jnp.dot(
        delta, dir_float[model_width:].T, precision=EXACT, preferred_element_type=jnp.float32
    )
    grad_arrived = jnp.zeros((arrived.shape[0], model_width), jnp.float32)
    grad_arrived = grad_arrived.at[pairs[:, 0]].add(grad_first).at[pairs[:, 1]].add(grad_second)
    returned = lax.all_to_all(
        grad_arrived.astype(jnp.bfloat16), "wide", split_axis=0, concat_axis=0, tiled=True
    )
    grad_picked = returned[slots].astype(jnp.float32)
    grad_encoded = (
        out_cotangent.reshape(-1, model_width).astype(jnp.float32).at[picked_rows].add(grad_picked)
    )
    grad_encoded = grad_encoded * allowed_rows
    grad_two, grad_second_gain, grad_second_shift = norm_backward(
        grad_encoded, normed_two, inverse_two, second_float
    )
    grad_lowered = grad_two.astype(jnp.bfloat16)
    grad_down_weight = jnp.einsum(
        "rf,rd->fd", active, grad_lowered, preferred_element_type=jnp.float32
    )
    grad_down_bias = jnp.sum(grad_lowered.astype(jnp.float32), 0)
    grad_active = jnp.einsum(
        "rd,fd->rf", grad_lowered, down_weight, preferred_element_type=jnp.float32
    )
    density = jnp.exp(-0.5 * upper_pre * upper_pre) * 0.3989422804014327
    grad_upper = (grad_active * (cumulative + upper_pre * density)).astype(jnp.bfloat16)
    grad_up_weight = jnp.einsum(
        "rd,rf->df", hidden_low, grad_upper, preferred_element_type=jnp.float32
    )
    grad_up_bias = jnp.sum(grad_upper.astype(jnp.float32), 0)
    grad_hidden = grad_two + jnp.einsum(
        "rf,df->rd", grad_upper, up_weight, preferred_element_type=jnp.float32
    )
    grad_one, grad_first_gain, grad_first_shift = norm_backward(
        grad_hidden, normed_one, inverse_one, first_gain.astype(jnp.float32)
    )
    grad_attended = grad_one.astype(jnp.bfloat16)
    grad_out_weight = jnp.einsum(
        "rd,re->de", mixed, grad_attended, preferred_element_type=jnp.float32
    )
    grad_out_bias = jnp.sum(grad_attended.astype(jnp.float32), 0)
    grad_mixed = jnp.einsum(
        "re,de->rd", grad_attended, out_weight, preferred_element_type=jnp.float32
    ).astype(jnp.bfloat16)
    grad_parts = []
    for doc_index in range(doc_count):
        doc_block = qkv[doc_index * length : (doc_index + 1) * length]
        queries = split_heads(doc_block, 0)
        key_rows = split_heads(doc_block, 1)
        value_rows = split_heads(doc_block, 2)
        scores = scores_of(queries, key_rows, allowed[doc_index])
        attention = jnp.exp(scores - log_totals[doc_index])
        grad_doc = grad_mixed[doc_index * length : (doc_index + 1) * length].reshape(
            length, HEADS, HEAD_DIM
        )
        grad_chance = jnp.einsum(
            "qhd,khd->hqk", grad_doc, value_rows, preferred_element_type=jnp.float32
        )
        inner = jnp.sum(grad_chance * attention, -1, keepdims=True)
        grad_scores = (attention * (grad_chance - inner)).astype(jnp.bfloat16)
        grad_query = (
            jnp.einsum("hqk,khd->qhd", grad_scores, key_rows, preferred_element_type=jnp.float32)
            * score_scale
        )
        grad_key = (
            jnp.einsum("hqk,qhd->khd", grad_scores, queries, preferred_element_type=jnp.float32)
            * score_scale
        )
        grad_value = jnp.einsum(
            "hqk,qhd->khd",
            attention.astype(jnp.bfloat16),
            grad_doc,
            preferred_element_type=jnp.float32,
        )
        grad_parts.append(
            jnp.concatenate(
                [
                    grad_query.reshape(length, model_width),
                    grad_key.reshape(length, model_width),
                    grad_value.reshape(length, model_width),
                ],
                axis=1,
            )
        )
    grad_qkv = jnp.concatenate(grad_parts).astype(jnp.bfloat16)
    grad_qkv_float = grad_qkv.astype(jnp.float32)
    grad_query_bias = jnp.sum(grad_qkv_float[:, :model_width], 0)
    grad_value_bias = jnp.sum(grad_qkv_float[:, 2 * model_width :], 0)
    grad_qkv_weight = jnp.einsum(
        "rd,re->de", token_rows, grad_qkv, preferred_element_type=jnp.float32
    )
    grad_tokens = (
        jnp.einsum("re,de->rd", grad_qkv, qkv_weight, preferred_element_type=jnp.float32) + grad_one
    ).astype(jnp.bfloat16)
    matrices = (grad_qkv_weight, grad_out_weight, grad_up_weight, grad_down_weight)
    partial_sums = (
        lax.psum_scatter(
            matrices[0].astype(jnp.bfloat16), "wide", scatter_dimension=1, tiled=True
        ).astype(jnp.float32),
        lax.psum_scatter(
            matrices[1].astype(jnp.bfloat16), "wide", scatter_dimension=1, tiled=True
        ).astype(jnp.float32),
        lax.psum_scatter(
            matrices[2].astype(jnp.bfloat16), "wide", scatter_dimension=1, tiled=True
        ).astype(jnp.float32),
        lax.psum_scatter(
            matrices[3].astype(jnp.bfloat16), "wide", scatter_dimension=1, tiled=True
        ).astype(jnp.float32),
    )
    summed_mats = (
        lax.psum_scatter(
            partial_sums[0].astype(jnp.bfloat16), "narrow", scatter_dimension=0, tiled=True
        ).astype(jnp.float32),
        lax.psum_scatter(
            partial_sums[1].astype(jnp.bfloat16), "narrow", scatter_dimension=0, tiled=True
        ).astype(jnp.float32),
        lax.psum_scatter(
            partial_sums[2].astype(jnp.bfloat16), "narrow", scatter_dimension=0, tiled=True
        ).astype(jnp.float32),
        lax.psum_scatter(
            partial_sums[3].astype(jnp.bfloat16), "narrow", scatter_dimension=0, tiled=True
        ).astype(jnp.float32),
    )
    smalls = lax.psum(
        (
            grad_query_bias,
            grad_value_bias,
            grad_out_bias,
            grad_first_gain,
            grad_first_shift,
            grad_up_bias,
            grad_down_bias,
            grad_second_gain,
            grad_second_shift,
            grad_dir_weight,
            grad_dir_bias,
        ),
        ("wide", "narrow"),
    )
    return (
        encoded_rows.reshape(tokens.shape),
        grad_tokens.reshape(tokens.shape),
        summed_mats[0],
        smalls[0],
        smalls[1],
        summed_mats[1],
        smalls[2],
        smalls[3],
        smalls[4],
        summed_mats[2],
        smalls[5],
        summed_mats[3],
        smalls[6],
        smalls[7],
        smalls[8],
        smalls[9],
        smalls[10],
    )


def solution(mesh):
    placed = (
        P(("wide", "narrow"), None, None),
        P(("wide", "narrow")),
        P(),
        P(),
        P(),
        P(),
        P(),
        P(),
        P(),
        P(),
        P(),
        P(),
        P(),
        P(),
        P(),
        P(),
        P(),
        P(("wide", "narrow"), None),
        P(("wide", "narrow"), None),
        P(("wide", "narrow"), None, None),
        P(("wide", "narrow"), None),
        P(("wide", "narrow"), None, None),
    )
    return jax.shard_map(
        on_device,
        mesh=mesh,
        in_specs=placed,
        out_specs=(
            P(("wide", "narrow"), None, None),
            P(("wide", "narrow"), None, None),
            P("narrow", "wide"),
            P(),
            P(),
            P("narrow", "wide"),
            P(),
            P(),
            P(),
            P("narrow", "wide"),
            P(),
            P("narrow", "wide"),
            P(),
            P(),
            P(),
            P(),
            P(),
        ),
        check_vma=False,
    )
```

profile of v0, /device:TPU:0, one launch (start us, length us, event | category | flops | bytes accessed | tf_op | source)
XLA Modules:
  0.0 747.2 jit_solution(5606578285930874321)
XLA Ops:
  20.7 5.9 add_convert_fusion
  66.9 13.4 %multiply_convert_fusion.2 = (bf16[1024,3072]{1,0:T(8,128)(2,1)S(1)}, f32[1024,3072]{1,0:T(8,128)}) fusion(f32[3072]{0:T(1024)S(1)} %copy-done.46, bf16[768,3072]{1,0:T(8,128)(2,1)} %param.31, f32[1024,768]{1,0:T(8,128)S(1)} %get-tuple-element.114, f32[768]{0:T(1024)S(1)} %copy-done.50, f32[768]{0:T(1024)S(1)} %convert_element_type.164, ...), kind=kOutput, calls=%fused_computation.22 | convolution fusion | flops 4854644736 | bytes 26765312 | tf_op jit(solution)/shard_map/dot_general | solution.py:111
  94.2 7.7 %all-to-all-start = ((bf16[8,32,768]{2,1,0:T(8,128)(2,1)}), bf16[8,32,768]{2,1,0:T(8,128)(2,1)}, u32[]{:S(2)}, u32[]{:S(2)}) async-start(bf16[8,32,768]{2,1,0:T(8,128)(2,1)} %bitcast.144), calls=%async_computation | async-start | bytes 786432 | tf_op jit(solution)/shard_map/all_to_all | solution.py:130
  105.0 8.6 %all-to-all-done = bf16[8,32,768]{2,1,0:T(8,128)(2,1)} async-done(((bf16[8,32,768]{2,1,0:T(8,128)(2,1)}), bf16[8,32,768]{2,1,0:T(8,128)(2,1)}, u32[]{:S(2)}, u32[]{:S(2)}) %all-to-all-start) | async-done | bytes 393248 | tf_op jit(solution)/shard_map/all_to_all | solution.py:130
  154.0 8.2 %scatter_custom_fusion.3 = f32[1024,768]{1,0:T(8,128)} fusion(f32[1024,768]{1,0:T(8,128)} %bitcast_convert_fusion, s32[256]{0:T(256)} %bitcast.154, bf16[256,768]{1,0:T(8,128)(2,1)} %bitcast.24, s32[1024]{0:T(1024)} %pad_clamp_fusion), kind=kCustom, calls=%fused_computation.84 | custom fusion | flops 393216 | bytes 3543040 | tf_op jit(solution)/shard_map/scatter-add | solution.py:169
  169.4 13.5 %convert_reduce_fusion = (f32[3072]{0:T(1024)}, bf16[1024,3072]{1,0:T(8,128)(2,1)S(1)}) fusion(f32[1024,3072]{1,0:T(8,128)} %get-tuple-element.116, f32[3072]{0:T(1024)S(1)} %copy-done.47, bf16[3072,768]{1,0:T(8,128)(2,1)S(1)} %bitcast.165, f32[1024,768]{1,0:T(8,128)S(1)} %get-tuple-element.94), kind=kOutput, calls=%fused_computation.15 | convolution fusion | flops 4873516032 | bytes 26763264 | tf_op jit(solution)/shard_map/rd,fd->rf/dot_general | solution.py:180
  182.9 6.5 multiply_reduce_fusion.3
  199.3 10.6 %multiply_reduce_fusion.1 = (f32[12,512]{1,0:T(8,128)S(1)}, f32[12,512,512]{1,2,0:T(8,128)}) fusion(f32[12,512,512]{1,2,0:T(8,128)} %copy-done.1, f32[12,512]{1,0:T(8,128)S(1)} %copy-done.28, bf16[512,12,64]{0,2,1:T(8,128)(2,1)S(1)} %bitcast.114, bf16[512,12,64]{0,2,1:T(8,128)(2,1)S(1)} %bitcast.131), kind=kOutput, calls=%fused_computation.20 | convolution fusion | flops 412084224 | bytes 26787840 | tf_op jit(solution)/shard_map/qhd,khd->hqk/dot_general | solution.py:214
  212.2 10.8 %multiply_convert_fusion.1 = bf16[12,512,512]{1,2,0:T(8,128)(2,1)} fusion(f32[12,512,512]{1,2,0:T(8,128)} %get-tuple-element.125, f32[12,512,512]{1,2,0:T(8,128)S(1)} %bitcast.104, f32[12,512]{1,0:T(8,128)S(1)} %get-tuple-element.124, f32[12,512]{1,0:T(8,128)S(1)} %copy-done.28), kind=kLoop, calls=%fused_computation.19 | loop fusion | flops 12582912 | bytes 31506432 | tf_op jit(solution)/shard_map/convert_element_type | solution.py:218
  236.7 6.7 multiply_reduce_fusion
  243.4 10.7 %multiply_convert_fusion = bf16[12,512,512]{1,2,0:T(8,128)(2,1)S(1)} fusion(f32[12,512,512]{1,2,0:T(8,128)} %get-tuple-element.123, f32[12,512,512]{1,2,0:T(8,128)} %copy-done.2, f32[12,512]{1,0:T(8,128)} %get-tuple-element.122, f32[12,512]{1,0:T(8,128)} %log_add_fusion), kind=kLoop, calls=%fused_computation.16 | loop fusion | flops 12582912 | bytes 31506432 | tf_op jit(solution)/shard_map/convert_element_type | solution.py:218
  260.8 29.7 %fusion.18 = bf16[768,2304]{0,1:T(8,128)(2,1)} fusion(bf16[1024,768]{1,0:T(8,128)(2,1)S(1)} %bitcast.170, bf16[512,768]{0,1:T(8,128)(2,1)S(1)} %bitcast.134, bf16[512,768]{0,1:T(8,128)(2,1)S(1)} %bitcast.141, bf16[512,768]{0,1:T(8,128)(2,1)S(1)} %bitcast.125, bf16[512,768]{0,1:T(8,128)(2,1)S(1)} %bitcast.135, bf16[512,768]{0,1:T(8,128)(2,1)S(1)} %bitcast.140, ...), kind=kOutput, calls=%fused_computation.45 | convolution fusion | flops 3653959680 | bytes 9830400 | tf_op jit(solution)/shard_map/rd,re->de/dot_general | solution.py:247
  290.6 10.7 %convolution_convert_fusion.1 = bf16[768,3072]{1,0:T(8,128)(2,1)} fusion(bf16[1024,3072]{1,0:T(8,128)(2,1)} %copy-done.63, f32[1024,768]{1,0:T(8,128)} %copy-done.6, f32[768]{0:T(1024)} %convert_element_type.165, f32[768]{0:T(1024)S(1)} %copy-done.42, f32[1024]{0:T(1024)} %copy-done.43, f32[1024]{0:T(1024)S(1)} %copy-done.40), kind=kOutput, calls=%fused_computation.42 | convolution fusion | flops 4838129664 | bytes 14170112 | tf_op jit(solution)/shard_map/rd,rf->df/dot_general | solution.py:185
  301.3 6.7 copy.105
  308.0 10.1 %convolution_convert_fusion = bf16[3072,768]{0,1:T(8,128)(2,1)} fusion(bf16[1024,3072]{1,0:T(8,128)(2,1)} %copy-done.64, f32[1024,768]{1,0:T(8,128)} %copy-done.22), kind=kOutput, calls=%fused_computation.41 | convolution fusion | flops 4834983936 | bytes 14155776 | tf_op jit(solution)/shard_map/rf,rd->fd/dot_general | solution.py:176
  320.0 68.3 %reduce-scatter.15.cloned.1.call-done = bf16[768,288]{0,1:T(8,128)(2,1)} async-done(((bf16[768,2304]{0,1:T(8,128)(2,1)}), bf16[768,288]{0,1:T(8,128)(2,1)}) %reduce-scatter.15.cloned.1.call-update) | async-done | bytes 442384 | tf_op jit(solution)/shard_map/reduce_scatter | solution.py:255
  390.5 96.5 %reduce-scatter.29.cloned.1.call-done = bf16[384,768]{1,0:T(8,128)(2,1)} async-done(((bf16[3072,768]{1,0:T(8,128)(2,1)}), bf16[384,768]{1,0:T(8,128)(2,1)}) %reduce-scatter.29.cloned.1.call-update) | async-done | bytes 589840
  492.9 92.7 %reduce-scatter.21.cloned.1.call-done = bf16[3072,96]{0,1:T(8,128)(2,1)} async-done(((bf16[3072,768]{0,1:T(8,128)(2,1)}), bf16[3072,96]{0,1:T(8,128)(2,1)}) %reduce-scatter.21.cloned.1.call-update) | async-done | bytes 589840 | tf_op jit(solution)/shard_map/reduce_scatter | solution.py:264
  587.3 7.3 fusion.54
  598.5 8.4 %add_convert_fusion.1 = bf16[1024,768]{1,0:T(8,128)(2,1)} fusion(f32[1024,768]{1,0:T(8,128)} %copy-done.25, bf16[768,2304]{1,0:T(8,128)(2,1)S(1)} %copy-done, bf16[512,768]{0,1:T(8,128)(2,1)} %bitcast.133, bf16[512,768]{0,1:T(8,128)(2,1)} %bitcast.143, bf16[512,768]{0,1:T(8,128)(2,1)} %bitcast.127, bf16[512,768]{0,1:T(8,128)(2,1)} %bitcast.137, ...), kind=kOutput, calls=%fused_computation.52 | convolution fusion | flops 3653763072 | bytes 12976128 | tf_op jit(solution)/shard_map/re,de->rd/dot_general | solution.py:251
  611.2 21.5 %reduce-scatter.25.cloned.1.call-done = bf16[192,288]{1,0:T(8,128)(2,1)} async-done(((bf16[768,288]{1,0:T(8,128)(2,1)}), bf16[192,288]{1,0:T(8,128)(2,1)}) %reduce-scatter.25.cloned.1.call-update) | async-done | bytes 110608
  636.1 21.3 %reduce-scatter.19.cloned.1.call-done = bf16[192,384]{1,0:T(8,128)(2,1)} async-done(((bf16[768,384]{1,0:T(8,128)(2,1)}), bf16[192,384]{1,0:T(8,128)(2,1)}) %reduce-scatter.19.cloned.1.call-update) | async-done | bytes 147472 | tf_op jit(solution)/shard_map/reduce_scatter | solution.py:275
  659.0 23.2 %reduce-scatter.23.cloned.1.call-done = bf16[768,96]{0,1:T(8,128)(2,1)} async-done(((bf16[3072,96]{0,1:T(8,128)(2,1)}), bf16[768,96]{0,1:T(8,128)(2,1)}) %reduce-scatter.23.cloned.1.call-update) | async-done | bytes 147472 | tf_op jit(solution)/shard_map/reduce_scatter | solution.py:278
  683.8 41.7 %all-reduce.3.cloned.1.call-done = (f32[768]{0:T(1024)}, f32[768]{0:T(1024)}, f32[768]{0:T(1024)}, f32[768]{0:T(1024)}, f32[768]{0:T(1024)}, /*index=5*/f32[3072...) async-done(((f32[768]{0:T(1024)}, f32[768]{0:T(1024)}, f32[768]{0:T(1024)}, f32[768]{0:T(1024)}, f32[768]{0:T(1024)}, ...) | async-done | bytes 86064 | tf_op jit(solution)/shard_map/psum | solution.py:282
  (286 shorter events, 189.9 us)
Async XLA Ops:
  11.0 69.3 %copy-start.41 = (f32[768]{0:T(1024)}, f32[768]{0:T(1024)S(1)}, u32[]{:S(2)}) copy-start(f32[768]{0:T(1024)S(1)} %convert_element_type.164) | copy-start | bytes 9220
  18.1 68.2 %copy-start.35 = (f32[1,4,2,128]{3,1,2,0:T(4,128)}, f32[1,4,2,128]{3,1,2,0:T(4,128)S(1)}, u32[]{:S(2)}) copy-start(f32[1,4,2,128]{3,1,2,0:T(4,128)S(1)} %copy.107) | copy-start | bytes 12292
  28.8 13.9 %copy-start.55 = (pred[512]{0:T(512)(128)(4,1)S(1)}, pred[512]{0:T(512)(128)(4,1)}, u32[]{:S(2)}) copy-start(pred[512]{0:T(512)(128)(4,1)} %get-tuple-element.78) | copy-start | bytes 1540
  66.2 14.0 %copy-start.6 = (f32[1024,768]{1,0:T(8,128)}, f32[1024,768]{1,0:T(8,128)S(1)}, u32[]{:S(2)}) copy-start(f32[1024,768]{1,0:T(8,128)S(1)} %get-tuple-element.114) | copy-start | bytes 9437188
  66.3 14.0 %copy-start.39 = (f32[1024]{0:T(1024)}, f32[1024]{0:T(1024)S(1)}, u32[]{:S(2)}) copy-start(f32[1024]{0:T(1024)S(1)} %broadcast_multiply_fusion.5) | copy-start | bytes 12292
  66.3 14.0 %slice-start.9 = ((s8[4718592]{0:T(1024)(128)(4,1)}), s8[4194304]{0:T(1024)(128)(4,1)S(1)}, s32[]{:S(2)}) async-start(s8[4718592]{0:T(1024)(128)(4,1)} %bitcast.162), calls=%async_computation.28 | async-start | bytes 8388608
  86.4 30.6 %copy-start.37 = (f32[1024]{0:T(1024)}, f32[1024]{0:T(1024)S(1)}, u32[]{:S(2)}) copy-start(f32[1024]{0:T(1024)S(1)} %add_rsqrt_fusion) | copy-start | bytes 12292
  94.2 19.4 %all-to-all-start = ((bf16[8,32,768]{2,1,0:T(8,128)(2,1)}), bf16[8,32,768]{2,1,0:T(8,128)(2,1)}, u32[]{:S(2)}, u32[]{:S(2)}) async-start(bf16[8,32,768]{2,1,0:T(8,128)(2,1)} %bitcast.144), calls=%async_computation | async-start | bytes 786432 | tf_op jit(solution)/shard_map/all_to_all | solution.py:130
  138.7 15.3 %all-to-all-start.1 = ((bf16[8,32,768]{2,1,0:T(8,128)(2,1)}), bf16[8,32,768]{2,1,0:T(8,128)(2,1)}, u32[]{:S(2)}, u32[]{:S(2)}) async-start(bf16[8,32,768]{2,1,0:T(8,128)(2,1)} %bitcast.145), calls=%async_computation.1 | async-start | bytes 786432 | tf_op jit(solution)/shard_map/all_to_all | solution.py:164
  142.8 175.4 %reduce-scatter.17.cloned.1.call-start = ((), (), s32[]{:S(2)}) async-start(), calls=%async_computation.11 | async-start | bytes 1327104 | tf_op jit(solution)/shard_map/reduce_scatter | solution.py:258
  167.4 15.4 %slice-start.13 = ((s8[4718592]{0:T(1024)(128)(4,1)}), s8[4194304]{0:T(1024)(128)(4,1)S(1)}, s32[]{:S(2)}) async-start(s8[4718592]{0:T(1024)(128)(4,1)} %bitcast.166), calls=%async_computation.32 | async-start | bytes 8388608
  169.3 13.5 %copy-start.22 = (f32[1024,768]{1,0:T(8,128)}, f32[1024,768]{1,0:T(8,128)S(1)}, u32[]{:S(2)}) copy-start(f32[1024,768]{1,0:T(8,128)S(1)} %get-tuple-element.94) | copy-start | bytes 9437188
  212.2 21.5 %slice-start.6 = ((s8[12582912]{0:T(1024)(128)(4,1)}), s8[4194304]{0:T(1024)(128)(4,1)S(1)}, s32[]{:S(2)}) async-start(s8[12582912]{0:T(1024)(128)(4,1)} %bitcast.107), calls=%async_computation.25 | async-start | bytes 8388608
  212.2 21.5 %slice-start.7 = ((s8[12582912]{0:T(1024)(128)(4,1)}), s8[4194304]{0:T(1024)(128)(4,1)S(1)}, s32[]{:S(2)}) async-start(s8[12582912]{0:T(1024)(128)(4,1)} %bitcast.107), calls=%async_computation.26 | async-start | bytes 8388608
  243.4 145.0 %reduce-scatter.15.cloned.1.call-start = ((), (), s32[]{:S(2)}) async-start(), calls=%async_computation.10 | async-start | bytes 3981312 | tf_op jit(solution)/shard_map/reduce_scatter | solution.py:255
  243.4 14.0 %slice-start.3 = ((s8[12582912]{0:T(1024)(128)(4,1)}), s8[4194304]{0:T(1024)(128)(4,1)S(1)}, s32[]{:S(2)}) async-start(s8[12582912]{0:T(1024)(128)(4,1)} %bitcast.105), calls=%async_computation.22 | async-start | bytes 8388608
  243.4 14.0 %slice-start.4 = ((s8[12582912]{0:T(1024)(128)(4,1)}), s8[4194304]{0:T(1024)(128)(4,1)S(1)}, s32[]{:S(2)}) async-start(s8[12582912]{0:T(1024)(128)(4,1)} %bitcast.105), calls=%async_computation.23 | async-start | bytes 8388608
  290.6 196.4 %reduce-scatter.29.cloned.1.call-start = ((), (), s32[]{:S(2)}) async-start(), calls=%async_computation.17 | async-start | bytes 5308416
  308.0 277.7 %reduce-scatter.21.cloned.1.call-start = ((), (), s32[]{:S(2)}) async-start(), calls=%async_computation.13 | async-start | bytes 5308416 | tf_op jit(solution)/shard_map/reduce_scatter | solution.py:264
  318.1 290.0 %reduce-scatter.27.cloned.1.call-start = ((), (), s32[]{:S(2)}) async-start(), calls=%async_computation.16 | async-start | bytes 245760
  320.0 312.7 %reduce-scatter.25.cloned.1.call-start = ((), (), s32[]{:S(2)}) async-start(), calls=%async_computation.15 | async-start | bytes 737280
  390.4 267.0 %reduce-scatter.19.cloned.1.call-start = ((), (), s32[]{:S(2)}) async-start(), calls=%async_computation.12 | async-start | bytes 737280 | tf_op jit(solution)/shard_map/reduce_scatter | solution.py:275
  489.1 193.1 %reduce-scatter.23.cloned.1.call-start = ((), (), s32[]{:S(2)}) async-start(), calls=%async_computation.14 | async-start | bytes 737280 | tf_op jit(solution)/shard_map/reduce_scatter | solution.py:278
  585.7 139.9 %all-reduce.3.cloned.1.call-start = ((), (), s32[]{:S(2)}) async-start(), calls=%async_computation.18 | async-start | bytes 189440 | tf_op jit(solution)/shard_map/psum | solution.py:282
  (67 other events, 387.4 us)
Sparse Core Ops, SparseCore 0:
  243.5 63.0 reduce-scatter.16
  310.2 78.0 reduce-scatter.14
  392.0 94.9 reduce-scatter.28
  490.5 95.1 reduce-scatter.20
  588.5 19.5 reduce-scatter.26
  610.5 22.1 reduce-scatter.24
  635.3 22.0 reduce-scatter.18
  660.1 22.0 reduce-scatter.22
Sparse Core Ops, SparseCore 1:
  598.5 126.9 all-reduce.2
where the time goes:
time: 756 us; the launch traced here: 747 us
  waiting for transfers between devices  379 us (50%)
  matrix products  170 us (22%)
  other arithmetic  94.5 us (12%)
  local copies, waits for them, and re-layouts  74.2 us (10%)
  between operations  16.8 us (2%)
  starting transfers between devices  12.4 us (2%)
    unnamed x12, waiting for transfers between devices  119 us
    reduce_scatter x1, waiting for transfers between devices, on_device(): lax.psum_scatter(matrices[3].astype(jnp.bfloat16), 'wide', scatter_dimens...  92.7 us
    reduce_scatter x1, waiting for transfers between devices, on_device(): lax.psum_scatter(matrices[0].astype(jnp.bfloat16), 'wide', scatter_dimens...  68.3 us
    unnamed x180, local copies, waits for them, and re-layouts  46 us
    psum x1, waiting for transfers between devices, on_device(): lax.psum((grad_query_bias, grad_value_bias, grad_out_bias, grad_first_gai...  41.7 us
    dot_general x1, matrix products, on_device(): jnp.einsum('rd,re->de', token_rows, grad_qkv, preferred_element_type=jnp....  29.7 us
    reduce_scatter x1, waiting for transfers between devices, on_device(): lax.psum_scatter(partial_sums[3].astype(jnp.bfloat16), 'narrow', scatter_...  23.2 us
    convert_element_type x2, other arithmetic, on_device(): grad_scores = (attention * (grad_chance - inner)).astype(jnp.bfloat16)  21.5 us
  transfers between devices with their start and end apart: 11, of which 10 were waited for; matrix products, arithmetic and copies ran while one was open for 16% of the time, Pallas kernels for 0%

commit v1 on v0

--- a/solution.py
+++ b/solution.py
@@ -280,20 +280,23 @@
         ).astype(jnp.float32),
     )
     smalls = lax.psum(
-        (
-            grad_query_bias,
-            grad_value_bias,
-            grad_out_bias,
-            grad_first_gain,
-            grad_first_shift,
-            grad_up_bias,
-            grad_down_bias,
-            grad_second_gain,
-            grad_second_shift,
-            grad_dir_weight,
-            grad_dir_bias,
+        lax.psum(
+            (
+                grad_query_bias,
+                grad_value_bias,
+                grad_out_bias,
+                grad_first_gain,
+                grad_first_shift,
+                grad_up_bias,
+                grad_down_bias,
+                grad_second_gain,
+                grad_second_shift,
+                grad_dir_weight,
+                grad_dir_bias,
+            ),
+            "narrow",
         ),
-        ("wide", "narrow"),
+        "wide",
     )
     return (
         encoded_rows.reshape(tokens.shape),

time: 756 us -> 790 us (1.045)
  waiting for transfers between devices: 379 us -> 415 us
    psum x0 -> x1, waiting for transfers between devices: none -> 76.6 us  [on_device(): lax.psum(lax.psum((grad_query_bias, grad_value_bias, grad_out_bias, grad_...]
    psum x1, waiting for transfers between devices: 41.7 us -> 0.03 us  [on_device(): lax.psum((grad_query_bias, grad_value_bias, grad_out_bias, grad_first_gai...]
    reduce_scatter x1, waiting for transfers between devices: 68.3 us -> 54.3 us  [on_device(): lax.psum_scatter(matrices[0].astype(jnp.bfloat16), 'wide', scatter_dimens...]
    unnamed x12 -> x13, waiting for transfers between devices: 119 us -> 132 us
  transfers between devices with their start and end apart: 11 -> 12, of which waited for: 10 -> 10; matrix products, arithmetic and copies ran while one was open for 16% -> 16% of each run, Pallas kernels for 0% -> 0%
where the time goes in v1:
time: 790 us; the launch traced here: 781 us
  waiting for transfers between devices  415 us (53%)
  matrix products  169 us (21%)
  other arithmetic  93.8 us (12%)
  local copies, waits for them, and re-layouts  74.1 us (9%)
  between operations  16.5 us (2%)
  starting transfers between devices  12.4 us (2%)
    unnamed x13, waiting for transfers between devices  132 us
    reduce_scatter x1, waiting for transfers between devices, on_device(): lax.psum_scatter(matrices[3].astype(jnp.bfloat16), 'wide', scatter_dimens...  96.4 us
    psum x1, waiting for transfers between devices, on_device(): lax.psum(lax.psum((grad_query_bias, grad_value_bias, grad_out_bias, grad_...  76.6 us
    reduce_scatter x1, waiting for transfers between devices, on_device(): lax.psum_scatter(matrices[0].astype(jnp.bfloat16), 'wide', scatter_dimens...  54.3 us
    unnamed x180, local copies, waits for them, and re-layouts  45.9 us
    dot_general x1, matrix products, on_device(): jnp.einsum('rd,re->de', token_rows, grad_qkv, preferred_element_type=jnp....  29.7 us
    reduce_scatter x1, waiting for transfers between devices, on_device(): lax.psum_scatter(partial_sums[3].astype(jnp.bfloat16), 'narrow', scatter_...  23 us
    convert_element_type x2, other arithmetic, on_device(): grad_scores = (attention * (grad_chance - inner)).astype(jnp.bfloat16)  21.5 us
  transfers between devices with their start and end apart: 12, of which 10 were waited for; matrix products, arithmetic and copies ran while one was open for 16% of the time, Pallas kernels for 0%

profile of v1, /device:TPU:0, one launch (start us, length us, event | category | flops | bytes accessed | tf_op | source)
XLA Modules:
  0.0 781.3 jit_solution(12315309381874402464)
XLA Ops:
  66.9 13.4 %multiply_convert_fusion.2 = (bf16[1024,3072]{1,0:T(8,128)(2,1)S(1)}, f32[1024,3072]{1,0:T(8,128)}) fusion(f32[3072]{0:T(1024)S(1)} %copy-done.46, bf16[768,3072]{1,0:T(8,128)(2,1)} %param.31, f32[1024,768]{1,0:T(8,128)S(1)} %get-tuple-element.125, f32[768]{0:T(1024)S(1)} %copy-done.50, f32[768]{0:T(1024)S(1)} %convert_element_type.164, ...), kind=kOutput, calls=%fused_computation.22 | convolution fusion | flops 4854644736 | bytes 26765312 | tf_op jit(solution)/shard_map/dot_general | solution.py:111
  94.3 7.7 all-to-all-start
  105.1 8.6 %all-to-all-done = bf16[8,32,768]{2,1,0:T(8,128)(2,1)} async-done(((bf16[8,32,768]{2,1,0:T(8,128)(2,1)}), bf16[8,32,768]{2,1,0:T(8,128)(2,1)}, u32[]{:S(2)}, u32[]{:S(2)}) %all-to-all-start) | async-done | bytes 393248 | tf_op jit(solution)/shard_map/all_to_all | solution.py:130
  154.1 8.2 %scatter_custom_fusion.3 = f32[1024,768]{1,0:T(8,128)} fusion(f32[1024,768]{1,0:T(8,128)} %bitcast_convert_fusion, s32[256]{0:T(256)} %bitcast.154, bf16[256,768]{1,0:T(8,128)(2,1)} %bitcast.24, s32[1024]{0:T(1024)} %pad_clamp_fusion), kind=kCustom, calls=%fused_computation.84 | custom fusion | flops 393216 | bytes 3543040 | tf_op jit(solution)/shard_map/scatter-add | solution.py:169
  169.4 13.4 %convert_reduce_fusion = (f32[3072]{0:T(1024)}, bf16[1024,3072]{1,0:T(8,128)(2,1)S(1)}) fusion(f32[1024,3072]{1,0:T(8,128)} %get-tuple-element.127, f32[3072]{0:T(1024)S(1)} %copy-done.47, bf16[3072,768]{1,0:T(8,128)(2,1)S(1)} %bitcast.165, f32[1024,768]{1,0:T(8,128)S(1)} %get-tuple-element.105), kind=kOutput, calls=%fused_computation.15 | convolution fusion | flops 4873516032 | bytes 26763264 | tf_op jit(solution)/shard_map/rd,fd->rf/dot_general | solution.py:180
  182.9 6.5 multiply_reduce_fusion.3
  199.3 10.6 %multiply_reduce_fusion.1 = (f32[12,512]{1,0:T(8,128)S(1)}, f32[12,512,512]{1,2,0:T(8,128)}) fusion(f32[12,512,512]{1,2,0:T(8,128)} %copy-done.1, f32[12,512]{1,0:T(8,128)S(1)} %copy-done.28, bf16[512,12,64]{0,2,1:T(8,128)(2,1)S(1)} %bitcast.114, bf16[512,12,64]{0,2,1:T(8,128)(2,1)S(1)} %bitcast.131), kind=kOutput, calls=%fused_computation.20 | convolution fusion | flops 412084224 | bytes 26787840 | tf_op jit(solution)/shard_map/qhd,khd->hqk/dot_general | solution.py:214
  212.2 10.8 %multiply_convert_fusion.1 = bf16[12,512,512]{1,2,0:T(8,128)(2,1)} fusion(f32[12,512,512]{1,2,0:T(8,128)} %get-tuple-element.136, f32[12,512,512]{1,2,0:T(8,128)S(1)} %bitcast.104, f32[12,512]{1,0:T(8,128)S(1)} %get-tuple-element.135, f32[12,512]{1,0:T(8,128)S(1)} %copy-done.28), kind=kLoop, calls=%fused_computation.19 | loop fusion | flops 12582912 | bytes 31506432 | tf_op jit(solution)/shard_map/convert_element_type | solution.py:218
  236.7 6.7 multiply_reduce_fusion
  243.4 10.7 %multiply_convert_fusion = bf16[12,512,512]{1,2,0:T(8,128)(2,1)S(1)} fusion(f32[12,512,512]{1,2,0:T(8,128)} %get-tuple-element.134, f32[12,512,512]{1,2,0:T(8,128)} %copy-done.2, f32[12,512]{1,0:T(8,128)} %get-tuple-element.133, f32[12,512]{1,0:T(8,128)} %log_add_fusion), kind=kLoop, calls=%fused_computation.16 | loop fusion | flops 12582912 | bytes 31506432 | tf_op jit(solution)/shard_map/convert_element_type | solution.py:218
  260.8 29.7 %fusion.18 = bf16[768,2304]{0,1:T(8,128)(2,1)} fusion(bf16[1024,768]{1,0:T(8,128)(2,1)S(1)} %bitcast.170, bf16[512,768]{0,1:T(8,128)(2,1)S(1)} %bitcast.134, bf16[512,768]{0,1:T(8,128)(2,1)S(1)} %bitcast.141, bf16[512,768]{0,1:T(8,128)(2,1)S(1)} %bitcast.125, bf16[512,768]{0,1:T(8,128)(2,1)S(1)} %bitcast.135, bf16[512,768]{0,1:T(8,128)(2,1)S(1)} %bitcast.140, ...), kind=kOutput, calls=%fused_computation.45 | convolution fusion | flops 3653959680 | bytes 9830400 | tf_op jit(solution)/shard_map/rd,re->de/dot_general | solution.py:247
  290.5 10.6 %convolution_convert_fusion.1 = bf16[768,3072]{1,0:T(8,128)(2,1)} fusion(bf16[1024,3072]{1,0:T(8,128)(2,1)} %copy-done.63, f32[1024,768]{1,0:T(8,128)} %copy-done.6, f32[768]{0:T(1024)} %convert_element_type.165, f32[768]{0:T(1024)S(1)} %copy-done.42, f32[1024]{0:T(1024)} %copy-done.43, f32[1024]{0:T(1024)S(1)} %copy-done.40), kind=kOutput, calls=%fused_computation.42 | convolution fusion | flops 4838129664 | bytes 14170112 | tf_op jit(solution)/shard_map/rd,rf->df/dot_general | solution.py:185
  301.2 6.6 copy.105
  307.9 10.1 %convolution_convert_fusion = bf16[3072,768]{0,1:T(8,128)(2,1)} fusion(bf16[1024,3072]{1,0:T(8,128)(2,1)} %copy-done.64, f32[1024,768]{1,0:T(8,128)} %copy-done.22), kind=kOutput, calls=%fused_computation.41 | convolution fusion | flops 4834983936 | bytes 14155776 | tf_op jit(solution)/shard_map/rf,rd->fd/dot_general | solution.py:176
  321.3 7.3 fusion.54
  334.3 54.3 %reduce-scatter.15.cloned.1.call-done = bf16[768,288]{0,1:T(8,128)(2,1)} async-done(((bf16[768,2304]{0,1:T(8,128)(2,1)}), bf16[768,288]{0,1:T(8,128)(2,1)}) %reduce-scatter.15.cloned.1.call-update) | async-done | bytes 442384 | tf_op jit(solution)/shard_map/reduce_scatter | solution.py:255
  390.8 96.3 %reduce-scatter.29.cloned.1.call-done = bf16[384,768]{1,0:T(8,128)(2,1)} async-done(((bf16[3072,768]{1,0:T(8,128)(2,1)}), bf16[384,768]{1,0:T(8,128)(2,1)}) %reduce-scatter.29.cloned.1.call-update) | async-done | bytes 589840
  489.3 96.4 %reduce-scatter.21.cloned.1.call-done = bf16[3072,96]{0,1:T(8,128)(2,1)} async-done(((bf16[3072,768]{0,1:T(8,128)(2,1)}), bf16[3072,96]{0,1:T(8,128)(2,1)}) %reduce-scatter.21.cloned.1.call-update) | async-done | bytes 589840 | tf_op jit(solution)/shard_map/reduce_scatter | solution.py:264
  586.4 8.4 %add_convert_fusion.1 = bf16[1024,768]{1,0:T(8,128)(2,1)} fusion(f32[1024,768]{1,0:T(8,128)} %copy-done.25, bf16[768,2304]{1,0:T(8,128)(2,1)S(1)} %copy-done, bf16[512,768]{0,1:T(8,128)(2,1)} %bitcast.133, bf16[512,768]{0,1:T(8,128)(2,1)} %bitcast.143, bf16[512,768]{0,1:T(8,128)(2,1)} %bitcast.127, bf16[512,768]{0,1:T(8,128)(2,1)} %bitcast.137, ...), kind=kOutput, calls=%fused_computation.52 | convolution fusion | flops 3653763072 | bytes 12976128 | tf_op jit(solution)/shard_map/re,de->rd/dot_general | solution.py:251
  594.8 13.3 %reduce-scatter.27.cloned.1.call-done = bf16[192,96]{1,0:T(8,128)(2,1)} async-done(((bf16[768,96]{1,0:T(8,128)(2,1)}), bf16[192,96]{1,0:T(8,128)(2,1)}) %reduce-scatter.27.cloned.1.call-update) | async-done | bytes 36880
  611.1 21.4 %reduce-scatter.25.cloned.1.call-done = bf16[192,288]{1,0:T(8,128)(2,1)} async-done(((bf16[768,288]{1,0:T(8,128)(2,1)}), bf16[192,288]{1,0:T(8,128)(2,1)}) %reduce-scatter.25.cloned.1.call-update) | async-done | bytes 110608
  635.9 21.2 %reduce-scatter.19.cloned.1.call-done = bf16[192,384]{1,0:T(8,128)(2,1)} async-done(((bf16[768,384]{1,0:T(8,128)(2,1)}), bf16[192,384]{1,0:T(8,128)(2,1)}) %reduce-scatter.19.cloned.1.call-update) | async-done | bytes 147472 | tf_op jit(solution)/shard_map/reduce_scatter | solution.py:275
  658.7 23.0 %reduce-scatter.23.cloned.1.call-done = bf16[768,96]{0,1:T(8,128)(2,1)} async-done(((bf16[3072,96]{0,1:T(8,128)(2,1)}), bf16[768,96]{0,1:T(8,128)(2,1)}) %reduce-scatter.23.cloned.1.call-update) | async-done | bytes 147472 | tf_op jit(solution)/shard_map/reduce_scatter | solution.py:278
  683.3 76.6 %all-reduce.5.cloned.1.call-done = (f32[768]{0:T(1024)}, f32[768]{0:T(1024)}, f32[768]{0:T(1024)}, f32[768]{0:T(1024)}, f32[768]{0:T(1024)}, /*index=5*/f32[3072...) async-done(((f32[768]{0:T(1024)}, f32[768]{0:T(1024)}, f32[768]{0:T(1024)}, f32[768]{0:T(1024)}, f32[768]{0:T(1024)}, ...) | async-done | bytes 86064 | tf_op jit(solution)/shard_map/psum | solution.py:282
  (289 shorter events, 193.0 us)
Async XLA Ops:
  11.1 69.3 %copy-start.41 = (f32[768]{0:T(1024)}, f32[768]{0:T(1024)S(1)}, u32[]{:S(2)}) copy-start(f32[768]{0:T(1024)S(1)} %convert_element_type.164) | copy-start | bytes 9220
  18.2 68.3 %copy-start.35 = (f32[1,4,2,128]{3,1,2,0:T(4,128)}, f32[1,4,2,128]{3,1,2,0:T(4,128)S(1)}, u32[]{:S(2)}) copy-start(f32[1,4,2,128]{3,1,2,0:T(4,128)S(1)} %copy.107) | copy-start | bytes 12292
  28.9 13.9 %copy-start.55 = (pred[512]{0:T(512)(128)(4,1)S(1)}, pred[512]{0:T(512)(128)(4,1)}, u32[]{:S(2)}) copy-start(pred[512]{0:T(512)(128)(4,1)} %get-tuple-element.78) | copy-start | bytes 1540
  66.3 14.0 %copy-start.6 = (f32[1024,768]{1,0:T(8,128)}, f32[1024,768]{1,0:T(8,128)S(1)}, u32[]{:S(2)}) copy-start(f32[1024,768]{1,0:T(8,128)S(1)} %get-tuple-element.125) | copy-start | bytes 9437188
  66.3 14.0 %copy-start.39 = (f32[1024]{0:T(1024)}, f32[1024]{0:T(1024)S(1)}, u32[]{:S(2)}) copy-start(f32[1024]{0:T(1024)S(1)} %broadcast_multiply_fusion.5) | copy-start | bytes 12292
  66.3 14.0 %slice-start.9 = ((s8[4718592]{0:T(1024)(128)(4,1)}), s8[4194304]{0:T(1024)(128)(4,1)S(1)}, s32[]{:S(2)}) async-start(s8[4718592]{0:T(1024)(128)(4,1)} %bitcast.162), calls=%async_computation.29 | async-start | bytes 8388608
  86.4 30.6 %copy-start.37 = (f32[1024]{0:T(1024)}, f32[1024]{0:T(1024)S(1)}, u32[]{:S(2)}) copy-start(f32[1024]{0:T(1024)S(1)} %add_rsqrt_fusion) | copy-start | bytes 12292
  94.3 19.4 %all-to-all-start = ((bf16[8,32,768]{2,1,0:T(8,128)(2,1)}), bf16[8,32,768]{2,1,0:T(8,128)(2,1)}, u32[]{:S(2)}, u32[]{:S(2)}) async-start(bf16[8,32,768]{2,1,0:T(8,128)(2,1)} %bitcast.144), calls=%async_computation | async-start | bytes 786432 | tf_op jit(solution)/shard_map/all_to_all | solution.py:130
  138.8 15.3 %all-to-all-start.1 = ((bf16[8,32,768]{2,1,0:T(8,128)(2,1)}), bf16[8,32,768]{2,1,0:T(8,128)(2,1)}, u32[]{:S(2)}, u32[]{:S(2)}) async-start(bf16[8,32,768]{2,1,0:T(8,128)(2,1)} %bitcast.145), calls=%async_computation.1 | async-start | bytes 786432 | tf_op jit(solution)/shard_map/all_to_all | solution.py:164
  142.9 189.6 %reduce-scatter.17.cloned.1.call-start = ((), (), s32[]{:S(2)}) async-start(), calls=%async_computation.11 | async-start | bytes 1327104 | tf_op jit(solution)/shard_map/reduce_scatter | solution.py:258
  167.4 15.4 %slice-start.13 = ((s8[4718592]{0:T(1024)(128)(4,1)}), s8[4194304]{0:T(1024)(128)(4,1)S(1)}, s32[]{:S(2)}) async-start(s8[4718592]{0:T(1024)(128)(4,1)} %bitcast.166), calls=%async_computation.33 | async-start | bytes 8388608
  212.2 21.5 %slice-start.6 = ((s8[12582912]{0:T(1024)(128)(4,1)}), s8[4194304]{0:T(1024)(128)(4,1)S(1)}, s32[]{:S(2)}) async-start(s8[12582912]{0:T(1024)(128)(4,1)} %bitcast.107), calls=%async_computation.26 | async-start | bytes 8388608
  212.2 21.5 %slice-start.7 = ((s8[12582912]{0:T(1024)(128)(4,1)}), s8[4194304]{0:T(1024)(128)(4,1)S(1)}, s32[]{:S(2)}) async-start(s8[12582912]{0:T(1024)(128)(4,1)} %bitcast.107), calls=%async_computation.27 | async-start | bytes 8388608
  243.4 145.3 %reduce-scatter.15.cloned.1.call-start = ((), (), s32[]{:S(2)}) async-start(), calls=%async_computation.10 | async-start | bytes 3981312 | tf_op jit(solution)/shard_map/reduce_scatter | solution.py:255
  243.4 14.0 %slice-start.3 = ((s8[12582912]{0:T(1024)(128)(4,1)}), s8[4194304]{0:T(1024)(128)(4,1)S(1)}, s32[]{:S(2)}) async-start(s8[12582912]{0:T(1024)(128)(4,1)} %bitcast.105), calls=%async_computation.23 | async-start | bytes 8388608
  243.4 14.0 %slice-start.4 = ((s8[12582912]{0:T(1024)(128)(4,1)}), s8[4194304]{0:T(1024)(128)(4,1)S(1)}, s32[]{:S(2)}) async-start(s8[12582912]{0:T(1024)(128)(4,1)} %bitcast.105), calls=%async_computation.24 | async-start | bytes 8388608
  290.5 196.7 %reduce-scatter.29.cloned.1.call-start = ((), (), s32[]{:S(2)}) async-start(), calls=%async_computation.17 | async-start | bytes 5308416
  307.8 277.9 %reduce-scatter.21.cloned.1.call-start = ((), (), s32[]{:S(2)}) async-start(), calls=%async_computation.13 | async-start | bytes 5308416 | tf_op jit(solution)/shard_map/reduce_scatter | solution.py:264
  318.0 268.0 %all-reduce.7.cloned.1.call-start = ((), (), s32[]{:S(2)}) async-start(), calls=%async_computation.19 | async-start | bytes 189440 | tf_op jit(solution)/shard_map/psum | solution.py:283
  332.4 275.6 %reduce-scatter.27.cloned.1.call-start = ((), (), s32[]{:S(2)}) async-start(), calls=%async_computation.16 | async-start | bytes 245760
  334.3 298.2 %reduce-scatter.25.cloned.1.call-start = ((), (), s32[]{:S(2)}) async-start(), calls=%async_computation.15 | async-start | bytes 737280
  390.8 266.3 %reduce-scatter.19.cloned.1.call-start = ((), (), s32[]{:S(2)}) async-start(), calls=%async_computation.12 | async-start | bytes 737280 | tf_op jit(solution)/shard_map/reduce_scatter | solution.py:275
  489.3 192.4 %reduce-scatter.23.cloned.1.call-start = ((), (), s32[]{:S(2)}) async-start(), calls=%async_computation.14 | async-start | bytes 737280 | tf_op jit(solution)/shard_map/reduce_scatter | solution.py:278
  585.7 174.2 %all-reduce.5.cloned.1.call-start = ((), (), s32[]{:S(2)}) async-start(), calls=%async_computation.18 | async-start | bytes 189440 | tf_op jit(solution)/shard_map/psum | solution.py:282
  (68 other events, 400.7 us)
Sparse Core Ops, SparseCore 0:
  243.5 63.3 reduce-scatter.16
  310.5 78.1 reduce-scatter.14
  392.3 94.7 reduce-scatter.28
  490.6 94.9 reduce-scatter.20
  588.5 19.4 reduce-scatter.26
  610.4 22.0 reduce-scatter.24
  635.0 22.0 reduce-scatter.18
  659.6 22.0 reduce-scatter.22
  687.3 72.6 all-reduce.4
Sparse Core Ops, SparseCore 1:
  332.5 31.9 all-reduce.6
